TPU v7x, 32 devices: a whole 2x2x4 slice. The times are simulated.
32 devices in a mesh: mkt: 8 (over z, y), draw: 4 (over x, core).
Axes of the slice: x: 2, y: 2, z: 4, core: 2. Of those that a mesh axis runs over, the one named last changes fastest.
Arguments:
- x_char: float32 [384, 56, 8], P('mkt'), may hold values from -2.5 to 2.5
- nu_draws: float32 [384, 8, 2048], P('mkt', None, 'draw'), may hold values from -3 to 3
- coef_sigma: float32 [8], replicated, may hold values from 0.3 to 1.2
- log_share: float32 [384, 56], P('mkt'), may hold values from -7 to -4.5
- counts: int32 [384], P('mkt'), may hold values from 28 to 56
Outputs:
- mean_util: float32 [384, 56], P('mkt')
- jacobian: float32 [384, 56, 56], P(('mkt', 'draw'))
- sup_norms: float32 [3], replicated
Inputs may be any that keep to these rules, and one draw needn't show every extreme that they name: Products 0 to counts - 1 of a market are valid; the other slots are padding.
All inputs are finite; a program needn't handle non-finite values. Where the computation divides by a largest or mean magnitude, that divisor is 1e-20 or more.
Results may differ from a plain program's by a relative error of at most 0.00013.
Values sent between devices are 32-bit elements; how exact they have to be, the bound alone decides.
A program may use at most 64 MiB of HBM per device.

v0:
```python
import jax
import jax.numpy as jnp
from jax import lax
from jax.sharding import PartitionSpec as P

ITERS = 3
step_cap = 0.25
epsilon = 1e-06


def market_terms(mean_util, scaled, nu_draws, usable, inverse, with_products):
    tastes = jnp.einsum("mjk,mkr->mjr", scaled, nu_draws, precision=lax.Precision.HIGHEST)
    raised = jnp.where(usable[:, :, None], jnp.exp(mean_util[:, :, None] + tastes), 0.0)
    chance = raised / (1.0 + jnp.sum(raised, axis=1, keepdims=True))
    shares = jnp.sum(chance, axis=2) * inverse
    if with_products:
        cross_sums = (
            jnp.einsum("mjr,mlr->mjl", chance, chance, precision=lax.Precision.HIGHEST) * inverse
        )
        return (shares, cross_sums)
    return shares


def evaluate(mean_util, scaled, nu_draws, usable, inverse, with_products):
    groups = mean_util.shape[0] // 8
    folded = (
        mean_util.reshape(groups, 8, mean_util.shape[1]),
        scaled.reshape(groups, 8, scaled.shape[1], scaled.shape[2]),
        nu_draws.reshape(groups, 8, nu_draws.shape[1], nu_draws.shape[2]),
        usable.reshape(groups, 8, usable.shape[1]),
    )

    def per_group(items):
        return market_terms(items[0], items[1], items[2], items[3], inverse, with_products)

    def unfold(member):
        return member.reshape((groups * 8,) + member.shape[2:])

    return jax.tree.map(unfold, lax.map(per_group, folded))


def contraction(log_share, shares, usable):
    return jnp.where(usable, log_share - jnp.log(jnp.where(usable, shares, 1.0)), 0.0)


def step_size(largest):
    return jnp.minimum(1.0, step_cap / (largest + epsilon))


def jacobian_rows(shares, cross_sums, usable):
    slots = shares.shape[1]
    divisor = jnp.where(usable, shares, 1.0)
    identity = jnp.eye(slots, dtype=jnp.float32)
    paired = usable[:, :, None] & usable[:, None, :]
    return jnp.where(paired, identity[None, :, :] - cross_sums / divisor[:, :, None], 0.0)


def whole_sweeps(
    mean_util, scaled, nu_draws, usable, log_share, inverse, total_fn, peak_fn, final_fn
):
    norms_list = []
    for sweep in range(ITERS):
        partial_value = evaluate(mean_util, scaled, nu_draws, usable, inverse, False)
        shares = total_fn(partial_value)
        change = contraction(log_share, shares, usable)
        largest = peak_fn(jnp.max(jnp.abs(change)))
        mean_util = mean_util + step_size(largest) * change
        norms_list.append(largest)
    partial_value, cross_part = evaluate(mean_util, scaled, nu_draws, usable, inverse, True)
    shares, summed = final_fn(partial_value, cross_part)
    return (mean_util, shares, summed, norms_list)


def shards(x_char, nu_draws, coef_sigma, log_share, counts):
    slots = log_share.shape[1]
    markets = log_share.shape[0]
    draw_count = lax.axis_size("draw")
    inverse = 1.0 / (nu_draws.shape[2] * draw_count)
    usable = jnp.arange(slots, dtype=jnp.int32)[None, :] < counts[:, None]
    scaled = x_char * coef_sigma[None, None, :]
    inside = jnp.sum(jnp.where(usable, jnp.exp(log_share), 0.0), axis=1)
    mean_util = jnp.where(usable, log_share - jnp.log(1.0 - inside)[:, None], 0.0)
    own_rows = markets // draw_count
    first_row = lax.axis_index("draw") * own_rows
    usable_own = lax.dynamic_slice_in_dim(usable, first_row, own_rows, 0)

    def total_market(partial_value):
        return lax.psum(partial_value, "draw")

    def peak_market(local):
        return lax.pmax(local, "mkt")

    def final_market(partial_value, cross_part):
        return lax.psum((partial_value, cross_part), "draw")

    mean_util, shares, cross_sums, norms_list = whole_sweeps(
        mean_util,
        scaled,
        nu_draws,
        usable,
        log_share,
        inverse,
        total_market,
        peak_market,
        final_market,
    )
    jacobian = jacobian_rows(
        lax.dynamic_slice_in_dim(shares, first_row, own_rows, 0),
        lax.dynamic_slice_in_dim(cross_sums, first_row, own_rows, 0),
        usable_own,
    )
    return (mean_util, jacobian, jnp.stack(norms_list))


def solution(mesh):
    return jax.shard_map(
        shards,
        mesh=mesh,
        in_specs=(P("mkt", None, None), P("mkt", None, "draw"), P(), P("mkt", None), P("mkt")),
        out_specs=(P("mkt", None), P(("mkt", "draw"), None, None), P()),
        check_vma=False,
    )
```

profile of v0, /device:TPU:0, one launch (start us, length us, event | category | flops | bytes accessed | tf_op | source)
XLA Modules:
  0.0 216.6 jit_solution(17408170341341090726)
XLA Ops:
  10.8 13.2 %while.42 = (s32[]{:T(128)}, f32[6,8,56]{2,1,0:T(8,128)S(1)}, pred[6,8,56]{2,1,0:T(8,128)(4,1)S(1)}, f32[6,8,56]{2,1,0:T(8,128)S(1)}, f32[6,8,56,8]{2,3,1,0:T(8,128)S(1)}, /*index=5*/f32[6,8,8,512]{3,2,1,0:T(8,128)}, s32[]{:T(128)}) while((s32[]{:T(128)}, f32[6,8,56]{2,1,0:T(8,128)S(1)}, pred[6,8,56]{2,1,0:T(8,128)(4,1)S(1)}, ...), condition=%wide.region_4.5_spmd, body=%wide.region_1.4_spmd.sunk | while | flops 23166976 | bytes 2085081 | solution.py:39
  10.9 2.0 fusion.44
  13.1 2.0 fusion.44
  15.3 2.0 fusion.44
  17.5 2.0 fusion.44
  24.0 12.9 %psum.35 = f32[48,56]{1,0:T(8,128)S(1)} all-reduce(f32[48,56]{1,0:T(8,128)S(1)} %bitcast.133), channel_id=1, replica_groups=mesh['mkt'=8,'draw'=4] {'draw'}, use_global_device_ids=true, to_apply=%region_5.6 | all-reduce | flops 2688 | bytes 21504 | tf_op jit(solution)/shard_map/psum | solution.py:88
  37.6 22.3 %pmax.21 = f32[]{:T(128)} all-reduce(f32[]{:T(128)} %abs_reduce_fusion.2), channel_id=1, replica_groups=mesh['mkt'=8,'draw'=4] {'mkt'}, use_global_device_ids=true, to_apply=%region_7.8 | all-reduce | flops 1 | bytes 8 | tf_op jit(solution)/shard_map/pmax | solution.py:91
  60.7 13.2 %while.43 = (s32[]{:T(128)}, f32[6,8,56]{2,1,0:T(8,128)S(1)}, pred[6,8,56]{2,1,0:T(8,128)(4,1)S(1)}, f32[6,8,56]{2,1,0:T(8,128)S(1)}, f32[6,8,56,8]{2,3,1,0:T(8,128)S(1)}, /*index=5*/f32[6,8,8,512]{3,2,1,0:T(8,128)}, s32[]{:T(128)}) while((s32[]{:T(128)}, f32[6,8,56]{2,1,0:T(8,128)S(1)}, pred[6,8,56]{2,1,0:T(8,128)(4,1)S(1)}, ...), condition=%wide.region_11.12_spmd, body=%wide.region_8.11_spmd.sunk | while | flops 23166976 | bytes 2085081 | solution.py:39
  60.7 2.0 fusion.45
  62.9 2.0 fusion.45
  65.1 2.0 fusion.45
  67.3 2.0 fusion.45
  69.5 2.0 fusion.45
  71.7 2.0 fusion.45
  73.9 10.3 %psum.36 = f32[48,56]{1,0:T(8,128)S(1)} all-reduce(f32[48,56]{1,0:T(8,128)S(1)} %bitcast.134), channel_id=1, replica_groups=mesh['mkt'=8,'draw'=4] {'draw'}, use_global_device_ids=true, to_apply=%region_12.13 | all-reduce | flops 2688 | bytes 21504 | tf_op jit(solution)/shard_map/psum | solution.py:88
  84.9 17.8 %pmax.22 = f32[]{:T(128)} all-reduce(f32[]{:T(128)} %get-tuple-element.192), channel_id=1, replica_groups=mesh['mkt'=8,'draw'=4] {'mkt'}, use_global_device_ids=true, to_apply=%region_14.15 | all-reduce | flops 1 | bytes 8 | tf_op jit(solution)/shard_map/pmax | solution.py:91
  103.4 13.2 %while.44 = (s32[]{:T(128)}, f32[6,8,56]{2,1,0:T(8,128)S(1)}, pred[6,8,56]{2,1,0:T(8,128)(4,1)S(1)}, f32[6,8,56]{2,1,0:T(8,128)S(1)}, f32[6,8,56,8]{2,3,1,0:T(8,128)S(1)}, /*index=5*/f32[6,8,8,512]{3,2,1,0:T(8,128)}, s32[]{:T(128)}) while((s32[]{:T(128)}, f32[6,8,56]{2,1,0:T(8,128)S(1)}, pred[6,8,56]{2,1,0:T(8,128)(4,1)S(1)}, ...), condition=%wide.region_18.19_spmd, body=%wide.region_15.18_spmd.sunk | while | flops 23166976 | bytes 2085081 | solution.py:39
  116.6 10.3 %psum.37 = f32[48,56]{1,0:T(8,128)S(1)} all-reduce(f32[48,56]{1,0:T(8,128)S(1)} %bitcast.135), channel_id=1, replica_groups=mesh['mkt'=8,'draw'=4] {'draw'}, use_global_device_ids=true, to_apply=%region_19.20 | all-reduce | flops 2688 | bytes 21504 | tf_op jit(solution)/shard_map/psum | solution.py:88
  127.6 19.8 %pmax.23 = f32[]{:T(128)} all-reduce(f32[]{:T(128)} %abs_reduce_fusion), channel_id=1, replica_groups=mesh['mkt'=8,'draw'=4] {'mkt'}, use_global_device_ids=true, to_apply=%region_21.22 | all-reduce | flops 1 | bytes 8 | tf_op jit(solution)/shard_map/pmax | solution.py:91
  148.0 23.3 %while.45 = (s32[]{:T(128)}, f32[6,8,56]{2,1,0:T(8,128)S(1)}, f32[6,8,56,56]{3,2,1,0:T(8,128)}, pred[6,8,56]{2,1,0:T(8,128)(4,1)S(1)}, f32[6,8,56]{2,1,0:T(8,128...) while((s32[]{:T(128)}, f32[6,8,56]{2,1,0:T(8,128)S(1)}, ...), condition=%wide.region_25.26_spmd, body=%wide.region_22.25_spmd.sunk | while | flops 177562112 | bytes 3248865 | solution.py:39
  167.5 2.0 fusion.47
  171.4 11.7 %psum.39 = f32[48,56]{1,0:T(8,128)S(1)} all-reduce(f32[48,56]{1,0:T(8,128)S(1)} %bitcast.132), channel_id=1, replica_groups=mesh['mkt'=8,'draw'=4] {'draw'}, use_global_device_ids=true, to_apply=%region_27.28 | all-reduce | flops 2688 | bytes 21504 | tf_op jit(solution)/shard_map/psum | solution.py:94
  183.1 2.5 %pad_maximum_fusion = f32[3]{0:T(128)} fusion(f32[1]{0:T(128)} %bitcast.34, f32[1]{0:T(128)} %bitcast.33, f32[1]{0:T(128)} %bitcast.32), kind=kLoop, calls=%fused_computation.77 | loop fusion | flops 6 | bytes 24 | tf_op jit(solution)/shard_map/stack | solution.py:112
  185.6 22.2 %all-reduce.2.cloned.1.call-done = f32[48,56,56]{2,1,0:T(8,128)} async-done(((f32[48,56,56]{2,1,0:T(8,128)}), f32[48,56,56]{2,1,0:T(8,128)}) %all-reduce.2.cloned.1.call-update) | async-done | bytes 602128 | tf_op jit(solution)/shard_map/psum | solution.py:94
  (169 shorter events, 47.8 us)
Async XLA Ops:
  7.2 200.7 %all-reduce.2.cloned.1.call-start = ((), (), s32[]{:S(2)}) async-start(), calls=%async_computation | async-start | bytes 2752512 | tf_op jit(solution)/shard_map/psum | solution.py:94
  10.8 26.1 %copy-start = (f32[48,56]{1,0:T(8,128)S(1)}, f32[48,56]{1,0:T(8,128)}, u32[]{:S(2)}) copy-start(f32[48,56]{1,0:T(8,128)} %param.16) | copy-start | bytes 32260
  10.8 26.1 %copy-start.2 = (s32[48]{0:T(128)S(1)}, s32[48]{0:T(128)}, u32[]{:S(2)}) copy-start(s32[48]{0:T(128)} %param.17) | copy-start | bytes 580
  171.3 38.4 %copy-start.1 = (f32[6,8,56]{2,1,0:T(8,128)}, f32[6,8,56]{2,1,0:T(8,128)S(1)}, u32[]{:S(2)}) copy-start(f32[6,8,56]{2,1,0:T(8,128)S(1)} %get-tuple-element.473) | copy-start | bytes 32260
Sparse Core Ops, SparseCore 0:
  171.5 36.2 all-reduce.1
where the time goes:
time: 218 us; the launch traced here: 217 us
  blocking collectives  105 us (48%)
  matrix products  57.1 us (26%)
  waiting for transfers between devices  22.2 us (10%)
  between operations  16.2 us (7%)
  other arithmetic  13.4 us (6%)
    pmax x3, blocking collectives, peak_market(): return lax.pmax(local, 'mkt')  59.9 us
    dot_general x24, matrix products, market_terms(): jnp.einsum('mjk,mkr->mjr', scaled, nu_draws, precision=lax.Precision.HIGH...  47 us
    psum x3, blocking collectives, total_market(): return lax.psum(partial_value, 'draw')  33.4 us
    psum x1, waiting for transfers between devices, final_market(): return lax.psum((partial_value, cross_part), 'draw')  22.2 us
    psum x1, blocking collectives, final_market(): return lax.psum((partial_value, cross_part), 'draw')  11.7 us
    dot_general x6, matrix products, market_terms(): jnp.einsum('mjr,mlr->mjl', chance, chance, precision=lax.Precision.HIGHEST)  10.1 us
  transfers between devices with their start and end apart: 1, of which 1 were waited for; matrix products, arithmetic and copies ran while one was open for 1% of the time, Pallas kernels for 0%

commit v1 on v0

--- a/solution.py
+++ b/solution.py
@@ -85,7 +85,7 @@
     usable_own = lax.dynamic_slice_in_dim(usable, first_row, own_rows, 0)
 
     def total_market(partial_value):
-        return lax.psum(partial_value, "draw")
+        return jnp.sum(lax.all_gather(partial_value, "draw"), axis=0)
 
     def peak_market(local):
         return lax.pmax(local, "mkt")

time: 218 us -> 203 us (0.931)
  blocking collectives: 105 us -> 88 us
    psum x3 -> x0, blocking collectives: 33.4 us -> none  [total_market(): return lax.psum(partial_value, 'draw')]
    all_gather x0 -> x3, blocking collectives: none -> 17 us  [total_market(): return jnp.sum(lax.all_gather(partial_value, 'draw'), axis=0)]
where the time goes in v1:
time: 203 us; the launch traced here: 202 us
  blocking collectives  88 us (43%)
  matrix products  57.1 us (28%)
  waiting for transfers between devices  24.2 us (12%)
  between operations  16.2 us (8%)
  other arithmetic  13.5 us (7%)
    pmax x3, blocking collectives, peak_market(): return lax.pmax(local, 'mkt')  60.3 us
    dot_general x24, matrix products, market_terms(): jnp.einsum('mjk,mkr->mjr', scaled, nu_draws, precision=lax.Precision.HIGH...  47 us
    psum x1, waiting for transfers between devices, final_market(): return lax.psum((partial_value, cross_part), 'draw')  24.2 us
    all_gather x3, blocking collectives, total_market(): return jnp.sum(lax.all_gather(partial_value, 'draw'), axis=0)  17 us
    psum x1, blocking collectives, final_market(): return lax.psum((partial_value, cross_part), 'draw')  10.7 us
    dot_general x6, matrix products, market_terms(): jnp.einsum('mjr,mlr->mjl', chance, chance, precision=lax.Precision.HIGHEST)  10.1 us
  transfers between devices with their start and end apart: 1, of which 1 were waited for; matrix products, arithmetic and copies ran while one was open for 1% of the time, Pallas kernels for 0%

profile of v1, /device:TPU:0, one launch (start us, length us, event | category | flops | bytes accessed | tf_op | source)
XLA Modules:
  0.0 201.8 jit_solution(15489625697948824821)
XLA Ops:
  10.8 13.2 %while.42 = (s32[]{:T(128)}, f32[6,8,56]{2,1,0:T(8,128)S(1)}, pred[6,8,56]{2,1,0:T(8,128)(4,1)S(1)}, f32[6,8,56]{2,1,0:T(8,128)S(1)}, f32[6,8,56,8]{2,3,1,0:T(8,128)S(1)}, /*index=5*/f32[6,8,8,512]{3,2,1,0:T(8,128)}, s32[]{:T(128)}) while((s32[]{:T(128)}, f32[6,8,56]{2,1,0:T(8,128)S(1)}, pred[6,8,56]{2,1,0:T(8,128)(4,1)S(1)}, ...), condition=%wide.region_4.5_spmd, body=%wide.region_1.4_spmd.sunk | while | flops 23166976 | bytes 2085081 | solution.py:39
  17.5 2.0 fusion.44
  24.0 6.3 %all_gather.9 = f32[4,48,56]{2,1,0:T(8,128)S(1)} all-gather(f32[1,48,56]{2,1,0:T(8,128)S(1)} %bitcast.133), channel_id=1, replica_groups=mesh['mkt'=8,'draw'=4] {'draw'}, dimensions={0}, use_global_device_ids=true | all-gather | bytes 53760 | tf_op jit(solution)/shard_map/all_gather | solution.py:88
  31.1 22.8 %pmax.21 = f32[]{:T(128)} all-reduce(f32[]{:T(128)} %abs_reduce_fusion.2), channel_id=1, replica_groups=mesh['mkt'=8,'draw'=4] {'mkt'}, use_global_device_ids=true, to_apply=%region_7.8 | all-reduce | flops 1 | bytes 8 | tf_op jit(solution)/shard_map/pmax | solution.py:91
  54.6 13.2 %while.43 = (s32[]{:T(128)}, f32[6,8,56]{2,1,0:T(8,128)S(1)}, pred[6,8,56]{2,1,0:T(8,128)(4,1)S(1)}, f32[6,8,56]{2,1,0:T(8,128)S(1)}, f32[6,8,56,8]{2,3,1,0:T(8,128)S(1)}, /*index=5*/f32[6,8,8,512]{3,2,1,0:T(8,128)}, s32[]{:T(128)}) while((s32[]{:T(128)}, f32[6,8,56]{2,1,0:T(8,128)S(1)}, pred[6,8,56]{2,1,0:T(8,128)(4,1)S(1)}, ...), condition=%wide.region_11.12_spmd, body=%wide.region_8.11_spmd.sunk | while | flops 23166976 | bytes 2085081 | solution.py:39
  54.7 2.0 fusion.45
  56.9 2.0 fusion.45
  59.1 2.0 fusion.45
  61.3 2.0 fusion.45
  67.8 5.3 %all_gather.10 = f32[4,48,56]{2,1,0:T(8,128)S(1)} all-gather(f32[1,48,56]{2,1,0:T(8,128)S(1)} %bitcast.134), channel_id=1, replica_groups=mesh['mkt'=8,'draw'=4] {'draw'}, dimensions={0}, use_global_device_ids=true | all-gather | bytes 53760 | tf_op jit(solution)/shard_map/all_gather | solution.py:88
  73.9 17.8 %pmax.22 = f32[]{:T(128)} all-reduce(f32[]{:T(128)} %get-tuple-element.192), channel_id=1, replica_groups=mesh['mkt'=8,'draw'=4] {'mkt'}, use_global_device_ids=true, to_apply=%region_14.15 | all-reduce | flops 1 | bytes 8 | tf_op jit(solution)/shard_map/pmax | solution.py:91
  92.4 13.2 %while.44 = (s32[]{:T(128)}, f32[6,8,56]{2,1,0:T(8,128)S(1)}, pred[6,8,56]{2,1,0:T(8,128)(4,1)S(1)}, f32[6,8,56]{2,1,0:T(8,128)S(1)}, f32[6,8,56,8]{2,3,1,0:T(8,128)S(1)}, /*index=5*/f32[6,8,8,512]{3,2,1,0:T(8,128)}, s32[]{:T(128)}) while((s32[]{:T(128)}, f32[6,8,56]{2,1,0:T(8,128)S(1)}, pred[6,8,56]{2,1,0:T(8,128)(4,1)S(1)}, ...), condition=%wide.region_18.19_spmd, body=%wide.region_15.18_spmd.sunk | while | flops 23166976 | bytes 2085081 | solution.py:39
  92.5 2.0 fusion.46
  105.6 5.3 %all_gather.11 = f32[4,48,56]{2,1,0:T(8,128)S(1)} all-gather(f32[1,48,56]{2,1,0:T(8,128)S(1)} %bitcast.135), channel_id=1, replica_groups=mesh['mkt'=8,'draw'=4] {'draw'}, dimensions={0}, use_global_device_ids=true | all-gather | bytes 53760 | tf_op jit(solution)/shard_map/all_gather | solution.py:88
  111.7 19.8 %pmax.23 = f32[]{:T(128)} all-reduce(f32[]{:T(128)} %abs_reduce_fusion), channel_id=1, replica_groups=mesh['mkt'=8,'draw'=4] {'mkt'}, use_global_device_ids=true, to_apply=%region_21.22 | all-reduce | flops 1 | bytes 8 | tf_op jit(solution)/shard_map/pmax | solution.py:91
  132.1 23.3 %while.45 = (s32[]{:T(128)}, f32[6,8,56]{2,1,0:T(8,128)S(1)}, f32[6,8,56,56]{3,2,1,0:T(8,128)}, pred[6,8,56]{2,1,0:T(8,128)(4,1)S(1)}, f32[6,8,56]{2,1,0:T(8,128...) while((s32[]{:T(128)}, f32[6,8,56]{2,1,0:T(8,128)S(1)}, ...), condition=%wide.region_25.26_spmd, body=%wide.region_22.25_spmd.sunk | while | flops 177562112 | bytes 3248865 | solution.py:39
  132.2 2.0 fusion.47
  136.0 2.0 fusion.47
  143.8 2.0 fusion.47
  147.7 2.0 fusion.47
  151.6 2.0 fusion.47
  155.5 10.7 %psum.15 = f32[48,56]{1,0:T(8,128)S(1)} all-reduce(f32[48,56]{1,0:T(8,128)S(1)} %bitcast.132), channel_id=1, replica_groups=mesh['mkt'=8,'draw'=4] {'draw'}, use_global_device_ids=true, to_apply=%region_27.28 | all-reduce | flops 2688 | bytes 21504 | tf_op jit(solution)/shard_map/psum | solution.py:94
  166.2 2.5 %pad_maximum_fusion = f32[3]{0:T(128)} fusion(f32[1]{0:T(128)} %bitcast.34, f32[1]{0:T(128)} %bitcast.33, f32[1]{0:T(128)} %bitcast.32), kind=kLoop, calls=%fused_computation.77 | loop fusion | flops 6 | bytes 24 | tf_op jit(solution)/shard_map/stack | solution.py:112
  168.7 24.2 %all-reduce.2.cloned.1.call-done = f32[48,56,56]{2,1,0:T(8,128)} async-done(((f32[48,56,56]{2,1,0:T(8,128)}), f32[48,56,56]{2,1,0:T(8,128)}) %all-reduce.2.cloned.1.call-update) | async-done | bytes 602128 | tf_op jit(solution)/shard_map/psum | solution.py:94
  (172 shorter events, 47.8 us)
Async XLA Ops:
  7.2 185.8 %all-reduce.2.cloned.1.call-start = ((), (), s32[]{:S(2)}) async-start(), calls=%async_computation | async-start | bytes 2752512 | tf_op jit(solution)/shard_map/psum | solution.py:94
  10.8 19.6 %copy-start = (f32[48,56]{1,0:T(8,128)S(1)}, f32[48,56]{1,0:T(8,128)}, u32[]{:S(2)}) copy-start(f32[48,56]{1,0:T(8,128)} %param.16) | copy-start | bytes 32260
  10.8 19.6 %copy-start.2 = (s32[48]{0:T(128)S(1)}, s32[48]{0:T(128)}, u32[]{:S(2)}) copy-start(s32[48]{0:T(128)} %param.17) | copy-start | bytes 580
  155.4 39.5 %copy-start.1 = (f32[6,8,56]{2,1,0:T(8,128)}, f32[6,8,56]{2,1,0:T(8,128)S(1)}, u32[]{:S(2)}) copy-start(f32[6,8,56]{2,1,0:T(8,128)S(1)} %get-tuple-element.473) | copy-start | bytes 32260
Sparse Core Ops, SparseCore 0:
  155.6 37.3 all-reduce.1
